TPU v7x, 32 devices: a whole 2x2x4 slice. The times are simulated.
32 devices in a mesh: grp: 2 (over x), kv: 16 (over z, y, core).
Axes of the slice: x: 2, y: 2, z: 4, core: 2. Of those that a mesh axis runs over, the one named last changes fastest.
Arguments:
- absorbed_query: bfloat16 [8, 128, 576], P('grp', 'kv'), parts along dimension 0, may hold values from -65 to 65
- latent_cache: bfloat16 [8, 32768, 576], P('grp', 'kv'), parts along dimension 0, may hold values from -6 to 6
- slot_position: int32 [8, 32768], P('grp', 'kv'), parts along dimension 0, may hold values from 0 to 32767, as said below
- context_lengths: int32 [8], P('grp'), parts along dimension 0, may hold values from 16384 to 32768, as said below
- value_up: bfloat16 [128, 512, 128], P('kv'), may hold values from -2.09375 to 2.09375
Outputs:
- attended: bfloat16 [8, 16384], P('grp', 'kv'), parts along dimension 0
There are 2 independent parts, one for each index of `grp`. A program takes and returns all parts, laid end to end along the dimension named above; an argument that names none is the same for every part. Nothing has to cross between parts.
Inputs may be any that keep to these rules, and one draw needn't show every extreme that they name: `slot_position`: each row is an ordering of 0 to 32767. `context_lengths`: some request holds exactly 32768 tokens.
All inputs are finite; a program needn't handle non-finite values.
Results may differ from a plain program's by a relative error of at most 0.0095.
Values may be sent and summed in bfloat16 or wider, within the bound.
A program may use at most 64 MiB of HBM per device.

v0:
```python
import jax
import jax.numpy as jnp
from jax import lax
from jax.sharding import PartitionSpec as P

softmax_scale = 192.0 ** (-0.5)
masked_score = -1e30


def local_softmax(queries, cache_rows, positions, lengths_here, latent):
    scores = (
        jnp.einsum("rhd,rtd->rht", queries, cache_rows, preferred_element_type=jnp.float32)
        * softmax_scale
    )
    usable = (positions < lengths_here[:, None])[:, None, :]
    row_peak = jnp.max(jnp.where(usable, scores, masked_score), axis=2)
    weights = jnp.where(usable, jnp.exp(scores - row_peak[:, :, None]), jnp.float32(0.0))
    row_total = jnp.sum(weights, axis=2)
    mixed_sum = jnp.einsum(
        "rht,rtl->rhl",
        weights.astype(jnp.bfloat16),
        cache_rows[:, :, :latent],
        preferred_element_type=jnp.float32,
    )
    return (row_peak, row_total, mixed_sum)


def shards(absorbed_query, latent_cache, slot_position, context_lengths, value_up):
    latent = value_up.shape[1]
    queries = lax.all_gather(absorbed_query, "kv", axis=1, tiled=True)
    row_peak, row_total, mixed_sum = local_softmax(
        queries, latent_cache, slot_position, context_lengths, latent
    )
    peaks_all, totals, mixed_all = (
        lax.all_to_all(row_peak[None], "kv", split_axis=2, concat_axis=0, tiled=True),
        lax.all_to_all(row_total[None], "kv", split_axis=2, concat_axis=0, tiled=True),
        lax.all_to_all(mixed_sum[None], "kv", split_axis=2, concat_axis=0, tiled=True),
    )
    global_peak = jnp.max(peaks_all, axis=0)
    factor = jnp.exp(peaks_all - global_peak[None])
    total_part = jnp.sum(totals * factor, axis=0)
    mixed_part = jnp.sum(mixed_all * factor[:, :, :, None], axis=0)
    latent_out = (mixed_part / total_part[:, :, None]).astype(jnp.bfloat16)
    projected = jnp.einsum(
        "rhl,hlv->rhv", latent_out, value_up, preferred_element_type=jnp.float32
    ).astype(jnp.bfloat16)
    return projected.reshape(projected.shape[0], -1)


def solution(mesh):
    return jax.shard_map(
        shards,
        mesh=mesh,
        in_specs=(
            P("grp", "kv", None),
            P("grp", "kv", None),
            P("grp", "kv"),
            P("grp"),
            P("kv", None, None),
        ),
        out_specs=P("grp", "kv"),
        check_vma=False,
    )
```

profile of v0, /device:TPU:0, one launch (start us, length us, event | category | flops | bytes accessed | tf_op | source)
XLA Modules:
  0.0 89.2 jit_solution(5720511521802271005)
XLA Ops:
  0.0 0.0 copy-start
  0.0 25.5 %all_gather.3 = bf16[4,128,576]{2,1,0:T(8,128)(2,1)S(1)} all-gather(bf16[4,8,576]{2,1,0:T(8,128)(2,1)} %param.5), channel_id=1, replica_groups=mesh['grp'=2,'kv'=16] {'kv'}, dimensions={1}, use_global_device_ids=true | all-gather | bytes 626688 | tf_op jit(solution)/shard_map/all_gather | solution.py:30
  25.5 0.8 broadcast_compare_fusion
  26.3 5.9 %select_reduce_fusion = (f32[4,128]{1,0:T(4,128)S(1)}, f32[4,128,2048]{2,1,0:T(8,128)S(1)}) fusion(pred[4,2048]{1,0:T(4,128)(4,1)S(1)} %broadcast_compare_fusion, bf16[4,128,576]{2,1,0:T(8,128)(2,1)S(1)} %all_gather.3, bf16[4,2048,576]{1,2,0:T(8,128)(2,1)} %param.6), kind=kOutput, calls=%fused_computation.3 | convolution fusion | flops 1211104768 | bytes 14231552 | tf_op jit(solution)/shard_map/rhd,rtd->rht/dot_general | solution.py:12
  32.2 0.0 copy-start.1
  32.2 1.9 %copy-done.1 = f32[4,128,2048]{2,1,0:T(8,128)} copy-done((f32[4,128,2048]{2,1,0:T(8,128)}, f32[4,128,2048]{2,1,0:T(8,128)S(1)}, u32[]{:S(2)}) %copy-start.1) | copy-done | bytes 4194328
  34.2 1.0 %fusion.2 = f32[4,128]{1,0:T(4,128)S(1)} fusion(f32[4,128,2048]{2,1,0:T(8,128)S(1)} %get-tuple-element.8, f32[4,128]{1,0:T(4,128)S(1)} %get-tuple-element.7, pred[4,2048]{1,0:T(4,128)(4,1)S(1)} %broadcast_compare_fusion), kind=kLoop, calls=%fused_computation.4 | loop fusion | flops 4193792 | bytes 4206592 | tf_op jit(solution)/shard_map/reduce_sum | solution.py:18
  35.2 0.7 copy.20
  35.9 3.5 %all-to-all-start.2 = ((f32[1,4,128]{1,0,2:T(1,128)}), f32[1,4,128]{1,0,2:T(1,128)S(1)}, u32[]{:S(2)}, u32[]{:S(2)}) async-start(f32[1,4,128]{1,0,2:T(1,128)} %copy.20), calls=%async_computation.2 | async-start | bytes 131072 | tf_op jit(solution)/shard_map/all_to_all | solution.py:36
  39.4 0.7 copy.18
  40.2 6.1 %all-to-all-done.2 = f32[1,4,128]{1,0,2:T(1,128)S(1)} async-done(((f32[1,4,128]{1,0,2:T(1,128)}), f32[1,4,128]{1,0,2:T(1,128)S(1)}, u32[]{:S(2)}, u32[]{:S(2)}) %all-to-all-start.2) | async-done | bytes 2080 | tf_op jit(solution)/shard_map/all_to_all | solution.py:36
  46.3 3.5 %all-to-all-start.1 = ((f32[1,4,128]{1,0,2:T(1,128)}), f32[1,4,128]{1,0,2:T(1,128)S(1)}, u32[]{:S(2)}, u32[]{:S(2)}) async-start(f32[1,4,128]{1,0,2:T(1,128)} %copy.18), calls=%async_computation.1 | async-start | bytes 131072 | tf_op jit(solution)/shard_map/all_to_all | solution.py:35
  49.8 7.6 %fusion.9 = f32[1,4,128,512]{3,2,1,0:T(8,128)S(1)} fusion(bf16[4,2048,576]{1,2,0:T(8,128)(2,1)} %param.6, f32[4,128,2048]{2,1,0:T(8,128)} %copy-done.1, f32[4,128]{1,0:T(4,128)S(1)} %get-tuple-element.7, pred[4,2048]{1,0:T(4,128)(4,1)S(1)} %broadcast_compare_fusion), kind=kOutput, calls=%fused_computation.10 | convolution fusion | flops 1077936128 | bytes 13641728 | tf_op jit(solution)/shard_map/rht,rtl->rhl/dot_general | solution.py:19
  57.4 1.7 %copy.16 = f32[1,4,128,512]{3,1,0,2:T(4,128)} copy(f32[1,4,128,512]{3,2,1,0:T(8,128)S(1)} %fusion.9) | data formatting | bytes 2097152 | tf_op jit(solution)/shard_map/broadcast_in_dim | solution.py:37
  59.1 0.0 all-to-all-done.1
  59.1 6.0 %all-to-all-start = ((f32[1,4,128,512]{3,1,0,2:T(4,128)}), f32[1,4,128,512]{3,1,0,2:T(4,128)S(1)}, u32[]{:S(2)}, u32[]{:S(2)}) async-start(f32[1,4,128,512]{3,1,0,2:T(4,128)} %copy.16), calls=%async_computation | async-start | bytes 2097152 | tf_op jit(solution)/shard_map/all_to_all | solution.py:37
  65.0 0.2 copy.24
  65.2 0.2 copy.23
  65.4 22.5 %all-to-all-done = f32[1,4,128,512]{3,1,0,2:T(4,128)S(1)} async-done(((f32[1,4,128,512]{3,1,0,2:T(4,128)}), f32[1,4,128,512]{3,1,0,2:T(4,128)S(1)}, u32[]{:S(2)}, u32[]{:S(2)}) %all-to-all-start) | async-done | bytes 1048608 | tf_op jit(solution)/shard_map/all_to_all | solution.py:37
  87.9 0.3 fusion.15
  88.2 0.1 divide_convert_fusion
  88.3 0.0 copy-done
  88.3 0.9 fusion.14
  (2 shorter events, 0.1 us)
Async XLA Ops:
  0.0 88.3 %copy-start = (bf16[8,512,128]{2,1,0:T(8,128)(2,1)S(1)}, bf16[8,512,128]{2,1,0:T(8,128)(2,1)}, u32[]{:S(2)}) copy-start(bf16[8,512,128]{2,1,0:T(8,128)(2,1)} %param.9) | copy-start | bytes 3145732
  32.2 1.9 %copy-start.1 = (f32[4,128,2048]{2,1,0:T(8,128)}, f32[4,128,2048]{2,1,0:T(8,128)S(1)}, u32[]{:S(2)}) copy-start(f32[4,128,2048]{2,1,0:T(8,128)S(1)} %get-tuple-element.8) | copy-start | bytes 12582916
  35.9 10.4 %all-to-all-start.2 = ((f32[1,4,128]{1,0,2:T(1,128)}), f32[1,4,128]{1,0,2:T(1,128)S(1)}, u32[]{:S(2)}, u32[]{:S(2)}) async-start(f32[1,4,128]{1,0,2:T(1,128)} %copy.20), calls=%async_computation.2 | async-start | bytes 131072 | tf_op jit(solution)/shard_map/all_to_all | solution.py:36
  46.3 12.8 %all-to-all-start.1 = ((f32[1,4,128]{1,0,2:T(1,128)}), f32[1,4,128]{1,0,2:T(1,128)S(1)}, u32[]{:S(2)}, u32[]{:S(2)}) async-start(f32[1,4,128]{1,0,2:T(1,128)} %copy.18), calls=%async_computation.1 | async-start | bytes 131072 | tf_op jit(solution)/shard_map/all_to_all | solution.py:35
  59.1 28.9 %all-to-all-start = ((f32[1,4,128,512]{3,1,0,2:T(4,128)}), f32[1,4,128,512]{3,1,0,2:T(4,128)S(1)}, u32[]{:S(2)}, u32[]{:S(2)}) async-start(f32[1,4,128,512]{3,1,0,2:T(4,128)} %copy.16), calls=%async_computation | async-start | bytes 2097152 | tf_op jit(solution)/shard_map/all_to_all | solution.py:37
where the time goes:
time: 90.8 us; the launch traced here: 89.2 us
  waiting for transfers between devices  28.6 us (31%)
  blocking collectives  25.5 us (28%)
  matrix products  14.3 us (16%)
  starting transfers between devices  13 us (14%)
  local copies, waits for them, and re-layouts  5.41 us (6%)
  other arithmetic  2.35 us (3%)
    all_gather x1, blocking collectives, shards(): queries = lax.all_gather(absorbed_query, 'kv', axis=1, tiled=True)  25.5 us
    all_to_all x1, waiting for transfers between devices, shards(): lax.all_to_all(mixed_sum[None], 'kv', split_axis=2, concat_axis=0, tiled=...  22.5 us
    dot_general x1, matrix products, local_softmax(): jnp.einsum('rht,rtl->rhl', weights.astype(jnp.bfloat16), cache_rows[:, :,...  7.58 us
    all_to_all x1, waiting for transfers between devices, shards(): lax.all_to_all(row_total[None], 'kv', split_axis=2, concat_axis=0, tiled=...  6.11 us
    all_to_all x1, starting transfers between devices, shards(): lax.all_to_all(mixed_sum[None], 'kv', split_axis=2, concat_axis=0, tiled=...  5.97 us
    dot_general x1, matrix products, local_softmax(): jnp.einsum('rhd,rtd->rht', queries, cache_rows, preferred_element_type=jn...  5.91 us
    all_to_all x1, starting transfers between devices, shards(): lax.all_to_all(row_peak[None], 'kv', split_axis=2, concat_axis=0, tiled=T...  3.5 us
    all_to_all x1, starting transfers between devices, shards(): lax.all_to_all(row_total[None], 'kv', split_axis=2, concat_axis=0, tiled=...  3.49 us
  transfers between devices with their start and end apart: 3, of which 2 were waited for; matrix products, arithmetic and copies ran while one was open for 12% of the time, Pallas kernels for 0%

commit v1 on v0

v1 whole, which is shorter than its diff:
```python
import functools

import jax
import jax.numpy as jnp
from jax import lax
from jax.experimental import pallas as pl
from jax.experimental.pallas import tpu as pltpu
from jax.sharding import PartitionSpec as P

softmax_scale = 192.0 ** (-0.5)
masked_score = -1e30
MESH = pl.DeviceIdType.MESH
LANES = 128


def merge(parts):
    peak = functools.reduce(jnp.maximum, [lse for _, lse in parts])
    factors = [jnp.exp(lse - peak) for _, lse in parts]
    total = sum(factors[1:], factors[0])
    inverse = 1.0 / total
    mixed = sum(
        [part * (f * inverse) for (part, _), f in zip(parts[1:], factors[1:])],
        parts[0][0] * (factors[0] * inverse),
    )
    return mixed, peak + jnp.log(total)


def packed(mixed, lse):
    lanes = lax.broadcasted_iota(jnp.int32, (mixed.shape[0], LANES), 1)
    high = lse.astype(jnp.bfloat16).astype(jnp.float32)
    rest = lse - high
    middle = rest.astype(jnp.bfloat16).astype(jnp.float32)
    low = rest - middle
    return mixed.astype(jnp.bfloat16), jnp.where(
        lanes == 0, high, jnp.where(lanes == 1, middle, low)
    ).astype(jnp.bfloat16)


def unpacked(ref, latent):
    mixed = ref[:, :latent].astype(jnp.float32)
    tail = ref[:, latent:].astype(jnp.float32)
    return mixed, (tail[:, 0:1] + tail[:, 1:2]) + tail[:, 2:3]


def kernel(
    depth, q_ref, k_hbm, pos_ref, len_ref, w_hbm, out_ref,
    kbuf, wbuf, qall, qrows, keep, keep_lse,
    send1, recv1, send2, recv2, send3, recv3, final,
    k_sem, w_sem, qs_sem, qr_sem, s_sem, r_sem,
):
    requests, heads_here, width = q_ref.shape
    latent = wbuf.shape[1]
    devices = 4 * depth
    heads = devices * heads_here
    me = lax.axis_index("kv")
    core, row, level = lax.rem(me, 2), lax.rem(me // 2, 2), me // 4

    def device(dc, dr, dl):
        c = 1 - core if dc else core
        r = 1 - row if dr else row
        l = lax.rem(level + dl, depth) if dl else level
        return {"kv": (l * 2 + r) * 2 + c}

    def slot(dc, dr, dl):
        return (dc * 2 + dr) * depth + dl

    for r in range(requests):
        pltpu.make_async_copy(k_hbm.at[r], kbuf.at[r], k_sem.at[r]).start()
    pltpu.make_async_copy(w_hbm, wbuf, w_sem).start()

    core_peer, row_peer = device(1, 0, 0), device(0, 1, 0)
    level_peers = [device(0, 0, k) for k in range(1, depth)]
    barrier = pltpu.get_barrier_semaphore()
    for peer in [core_peer, row_peer] + level_peers:
        pl.semaphore_signal(barrier, inc=1, device_id=peer, device_id_type=MESH)
    pl.semaphore_wait(barrier, depth + 1)

    sends, arrivals = [], {}

    def send_query(src, place, peer):
        copy = pltpu.make_async_remote_copy(
            src_ref=src, dst_ref=qall.at[place],
            send_sem=qs_sem.at[place], recv_sem=qr_sem.at[place],
            device_id=peer, device_id_type=MESH,
        )
        copy.start()
        sends.append(copy)
        arrivals[place] = copy

    for k in range(1, depth):
        send_query(q_ref, slot(0, 0, (depth - k) % depth), level_peers[k - 1])
    send_query(q_ref, slot(0, 1, 0), row_peer)
    send_query(q_ref, slot(1, 0, 0), core_peer)
    qall[0] = q_ref[...]
    for k in range(1, depth):
        arrivals[slot(0, 0, k)].wait_recv()
        send_query(qall.at[slot(0, 0, k)], slot(0, 1, k), row_peer)
        send_query(qall.at[slot(0, 0, k)], slot(1, 0, k), core_peer)
    for k in range(depth):
        arrivals[slot(0, 1, k)].wait_recv()
        send_query(qall.at[slot(0, 1, k)], slot(1, 1, k), core_peer)
    for dr in range(2):
        for k in range(depth):
            arrivals[slot(1, dr, k)].wait_recv()

    def attend(r):
        for place in range(devices):
            qrows[place * heads_here : (place + 1) * heads_here, :] = qall[place, r].astype(jnp.float32)
        pltpu.make_async_copy(k_hbm.at[r], kbuf.at[r], k_sem.at[r]).wait()
        queries = qrows[...].astype(jnp.bfloat16)
        scores = lax.dot_general(
            queries, kbuf[r], (((1,), (1,)), ((), ())), preferred_element_type=jnp.float32
        )
        usable = pos_ref[r : r + 1, :] < len_ref[r]
        scores = jnp.where(usable, scores, masked_score)
        peak = jnp.max(scores, axis=1, keepdims=True)
        weights = jnp.exp((scores - peak) * softmax_scale)
        total = jnp.sum(weights, axis=1, keepdims=True)
        mixed = jnp.dot(
            weights.astype(jnp.bfloat16), kbuf[r, :, :latent], preferred_element_type=jnp.float32
        )
        return mixed * (1.0 / total), peak * softmax_scale + jnp.log(total)

    def send_part(src, dst, number, r, peer):
        copy = pltpu.make_async_remote_copy(
            src_ref=src, dst_ref=dst,
            send_sem=s_sem.at[number, r], recv_sem=r_sem.at[number, r],
            device_id=peer, device_id_type=MESH,
        )
        copy.start()
        sends.append(copy)
        return copy

    half, quarter = heads // 2, heads // 4
    first, second, third = {}, {}, {}

    def stage1(r):
        mixed, lse = attend(r)
        values, tail = packed(mixed[half:], lse[half:])
        send1[r, :, :latent] = values
        send1[r, :, latent:] = tail
        first[r] = send_part(send1.at[r], recv1.at[r], 0, r, core_peer)
        keep[r] = mixed[:half]
        keep_lse[r] = jnp.broadcast_to(lse[:half], (half, LANES))

    def stage2(r):
        first[r].wait_recv()
        mixed, lse = merge([(keep[r], keep_lse[r, :, 0:1]), unpacked(recv1.at[r], latent)])
        values, tail = packed(mixed[quarter:], lse[quarter:])
        send2[r, :, :latent] = values
        send2[r, :, latent:] = tail
        second[r] = send_part(send2.at[r], recv2.at[r], 1, r, row_peer)
        keep[r, :quarter] = mixed[:quarter]
        keep_lse[r, :quarter] = jnp.broadcast_to(lse[:quarter], (quarter, LANES))

    def stage3(r):
        second[r].wait_recv()
        mixed, lse = merge(
            [(keep[r, :quarter], keep_lse[r, :quarter, 0:1]), unpacked(recv2.at[r], latent)]
        )
        values, tail = packed(mixed, lse)
        for k in range(1, depth):
            rows = slice(k * heads_here, (k + 1) * heads_here)
            send3[r, k, :, :latent] = values[rows]
            send3[r, k, :, latent:] = tail[rows]
        for k in range(1, depth):
            third[r, k] = send_part(
                send3.at[r, k], recv3.at[r, depth - k], 1 + k, r, level_peers[k - 1]
            )
        keep[r, :heads_here] = mixed[:heads_here]
        keep_lse[r, :heads_here] = jnp.broadcast_to(lse[:heads_here], (heads_here, LANES))

    def stage4(r):
        parts = [(keep[r, :heads_here], keep_lse[r, :heads_here, 0:1])]
        for k in range(1, depth):
            third[r, k].wait_recv()
        for k in range(1, depth):
            parts.append(unpacked(recv3.at[r, k], latent))
        final[r] = merge(parts)[0]

    stages = [stage1, stage2, stage3, stage4]
    for step in range(requests + len(stages) - 1):
        for number, stage in enumerate(stages):
            if 0 <= step - number < requests:
                stage(step - number)

    pltpu.make_async_copy(w_hbm, wbuf, w_sem).wait()
    for h in range(heads_here):
        rows = final[:, h, :].astype(jnp.bfloat16)
        out_ref[:, h * wbuf.shape[2] : (h + 1) * wbuf.shape[2]] = jnp.dot(
            rows, wbuf[h], preferred_element_type=jnp.float32
        ).astype(out_ref.dtype)
    for copy in sends:
        copy.wait_send()


def shards(devices, absorbed_query, latent_cache, slot_position, context_lengths, value_up):
    depth = devices // 4
    requests, heads_here, width = absorbed_query.shape
    slots = latent_cache.shape[1]
    latent, value = value_up.shape[1:]
    heads = devices * heads_here
    wide = latent + LANES
    half, quarter = heads // 2, heads // 4
    vmem = pl.BlockSpec(memory_space=pltpu.VMEM)
    hbm = pl.BlockSpec(memory_space=pltpu.HBM)
    bf16, f32 = jnp.bfloat16, jnp.float32
    return pl.pallas_call(
        functools.partial(kernel, depth),
        out_shape=jax.ShapeDtypeStruct((requests, heads_here * value), bf16),
        in_specs=[vmem, hbm, vmem, pl.BlockSpec(memory_space=pltpu.SMEM), hbm],
        out_specs=vmem,
        scratch_shapes=[
            pltpu.VMEM((requests, slots, width), bf16),
            pltpu.VMEM(value_up.shape, bf16),
            pltpu.VMEM((devices, requests, heads_here, width), bf16),
            pltpu.VMEM((heads, width), f32),
            pltpu.VMEM((requests, half, latent), f32),
            pltpu.VMEM((requests, half, LANES), f32),
            pltpu.VMEM((requests, half, wide), bf16),
            pltpu.VMEM((requests, half, wide), bf16),
            pltpu.VMEM((requests, quarter, wide), bf16),
            pltpu.VMEM((requests, quarter, wide), bf16),
            pltpu.VMEM((requests, depth, heads_here, wide), bf16),
            pltpu.VMEM((requests, depth, heads_here, wide), bf16),
            pltpu.VMEM((requests, heads_here, latent), f32),
            pltpu.SemaphoreType.DMA((requests,)),
            pltpu.SemaphoreType.DMA,
            pltpu.SemaphoreType.DMA((devices,)),
            pltpu.SemaphoreType.DMA((devices,)),
            pltpu.SemaphoreType.DMA((1 + depth, requests)),
            pltpu.SemaphoreType.DMA((1 + depth, requests)),
        ],
        compiler_params=pltpu.CompilerParams(
            collective_id=0, has_side_effects=True, vmem_limit_bytes=56 * 1024 * 1024
        ),
        name="attention_step",
    )(absorbed_query, latent_cache, slot_position, context_lengths, value_up)


def solution(mesh):
    return jax.shard_map(
        functools.partial(shards, mesh.shape["kv"]),
        mesh=mesh,
        in_specs=(
            P("grp", "kv", None),
            P("grp", "kv", None),
            P("grp", "kv"),
            P("grp"),
            P("kv", None, None),
        ),
        out_specs=P("grp", "kv"),
        check_vma=False,
    )
```

time: 90.8 us -> 50 us (0.55); the launches traced: 89.2 us -> 49.4 us
  Pallas kernels: 0 us -> 34 us
  waiting for transfers between devices: 28.6 us -> 0 us
  blocking collectives: 25.5 us -> 0 us
  matrix products: 14.3 us -> 0 us
  starting transfers between devices: 13 us -> 0 us
  local copies, waits for them, and re-layouts: 5.41 us -> 15.4 us
  other arithmetic: 2.35 us -> 0 us
    pallas_call x0 -> x1, Pallas kernels: none -> 34 us  [shards(): pl.pallas_call(functools.partial(kernel, depth), out_shape=jax.ShapeDtype...]
    all_to_all x3 -> x0, waiting for transfers between devices: 28.6 us -> none  [the longest x1 22.5 us: shards(): lax.all_to_all(mixed_sum[None], 'kv', split_axis=2, concat_axis=0, tiled=...]
    all_gather x1 -> x0, blocking collectives: 25.5 us -> none  [shards(): queries = lax.all_gather(absorbed_query, 'kv', axis=1, tiled=True)]
    dot_general x3 -> x0, matrix products: 14.3 us -> none  [the longest x1 7.58 us: local_softmax(): jnp.einsum('rht,rtl->rhl', weights.astype(jnp.bfloat16), cache_rows[:, :,...]
    unnamed x4 -> x2, local copies, waits for them, and re-layouts: 1.93 us -> 15.4 us
    all_to_all x3 -> x0, starting transfers between devices: 13 us -> none  [the longest x1 5.97 us: shards(): lax.all_to_all(mixed_sum[None], 'kv', split_axis=2, concat_axis=0, tiled=...]
    broadcast_in_dim x3 -> x0, local copies, waits for them, and re-layouts: 3.15 us -> none  [the longest x1 1.67 us: shards(): mixed_sum[None]]
    reduce_sum x3 -> x0, other arithmetic: 1.4 us -> none  [the longest x1 1.04 us: local_softmax(): row_total = jnp.sum(weights, axis=2)]
  transfers between devices with their start and end apart: 3 -> 0, of which waited for: 2 -> 0; matrix products, arithmetic and copies ran while one was open for 12% -> 0% of each run, Pallas kernels for 0% -> 0%
where the time goes in v1:
time: 50 us; the launch traced here: 49.4 us
  Pallas kernels  34 us (68%)
  local copies, waits for them, and re-layouts  15.4 us (31%)
    pallas_call x1, Pallas kernels, shards(): pl.pallas_call(functools.partial(kernel, depth), out_shape=jax.ShapeDtype...  34 us
    unnamed x2, local copies, waits for them, and re-layouts  15.4 us

profile of v1, /device:TPU:0, one launch (start us, length us, event | category | flops | bytes accessed | tf_op | source)
XLA Modules:
  0.0 49.4 jit_solution(9643369188890126909)
XLA Ops:
  0.0 14.1 %copy.6.k_hbm = bf16[4,2048,576]{2,1,0:T(8,128)(2,1)} copy(bf16[4,2048,576]{1,2,0:T(8,128)(2,1)} %param.6) | data formatting | bytes 18874368 | tf_op args[1]
  14.1 34.0 %attention_step.1 = bf16[4,1024]{1,0:T(4,128)(2,1)} custom-call(bf16[4,8,576]{2,1,0:T(8,128)(2,1)} %q_ref.1, bf16[4,2048,576]{2,1,0:T(8,128)(2,1)} %copy.6.k_hbm, s32[4,2048]{1,0:T(4,128)} %pos_ref.1, s32[4]{0:T(128)} %len_ref.1, bf16[8,512,128]{2,1,0:T(8,128)(2,1)} %w_hbm.1), custom_call_target="tpu_custom_call" | custom-call | tf_op jit(solution)/shard_map/attention_step/pallas_call | solution.py:208
  48.1 1.3 %copy.8 = bf16[4,1024]{1,0:T(4,128)(2,1)} copy(bf16[4,1024]{1,0:T(4,128)(2,1)} %attention_step.1) | data formatting | bytes 16384

commit v2 on v1

--- a/solution.py
+++ b/solution.py
@@ -109,15 +109,18 @@
         pltpu.make_async_copy(k_hbm.at[r], kbuf.at[r], k_sem.at[r]).wait()
         queries = qrows[...].astype(jnp.bfloat16)
         scores = lax.dot_general(
-            queries, kbuf[r], (((1,), (1,)), ((), ())), preferred_element_type=jnp.float32
+            queries, kbuf[r], (((1,), (0,)), ((), ())), preferred_element_type=jnp.float32
         )
         usable = pos_ref[r : r + 1, :] < len_ref[r]
         scores = jnp.where(usable, scores, masked_score)
         peak = jnp.max(scores, axis=1, keepdims=True)
         weights = jnp.exp((scores - peak) * softmax_scale)
         total = jnp.sum(weights, axis=1, keepdims=True)
-        mixed = jnp.dot(
-            weights.astype(jnp.bfloat16), kbuf[r, :, :latent], preferred_element_type=jnp.float32
+        mixed = lax.dot_general(
+            weights.astype(jnp.bfloat16),
+            kbuf[r, :latent, :],
+            (((1,), (1,)), ((), ())),
+            preferred_element_type=jnp.float32,
         )
         return mixed * (1.0 / total), peak * softmax_scale + jnp.log(total)
 
@@ -211,7 +214,7 @@
         in_specs=[vmem, hbm, vmem, pl.BlockSpec(memory_space=pltpu.SMEM), hbm],
         out_specs=vmem,
         scratch_shapes=[
-            pltpu.VMEM((requests, slots, width), bf16),
+            pltpu.VMEM((requests, width, slots), bf16),
             pltpu.VMEM(value_up.shape, bf16),
             pltpu.VMEM((devices, requests, heads_here, width), bf16),
             pltpu.VMEM((heads, width), f32),
@@ -235,7 +238,7 @@
             collective_id=0, has_side_effects=True, vmem_limit_bytes=56 * 1024 * 1024
         ),
         name="attention_step",
-    )(absorbed_query, latent_cache, slot_position, context_lengths, value_up)
+    )(absorbed_query, jnp.swapaxes(latent_cache, 1, 2), slot_position, context_lengths, value_up)
 
 
 def solution(mesh):

time: 50 us -> 35.5 us (0.71)
  local copies, waits for them, and re-layouts: 15.4 us -> 1.3 us
    unnamed x2 -> x1, local copies, waits for them, and re-layouts: 15.4 us -> 1.3 us
where the time goes in v2:
time: 35.5 us; the launch traced here: 35.3 us
  Pallas kernels  34 us (96%)
  local copies, waits for them, and re-layouts  1.3 us (4%)
    pallas_call x1, Pallas kernels, shards(): pl.pallas_call(functools.partial(kernel, depth), out_shape=jax.ShapeDtype...  34 us
    unnamed x1, local copies, waits for them, and re-layouts  1.3 us

profile of v2, /device:TPU:0, one launch (start us, length us, event | category | flops | bytes accessed | tf_op | source)
XLA Modules:
  0.0 35.3 jit_solution(10940575425275307894)
XLA Ops:
  0.0 34.0 %attention_step.1 = bf16[4,1024]{1,0:T(4,128)(2,1)} custom-call(bf16[4,8,576]{2,1,0:T(8,128)(2,1)} %q_ref.1, bf16[4,576,2048]{2,1,0:T(8,128)(2,1)} %bitcast.1, s32[4,2048]{1,0:T(4,128)} %pos_ref.1, s32[4]{0:T(128)} %len_ref.1, bf16[8,512,128]{2,1,0:T(8,128)(2,1)} %w_hbm.1), custom_call_target="tpu_custom_call" | custom-call | tf_op jit(solution)/shard_map/attention_step/pallas_call | solution.py:211
  34.0 1.3 %copy.7 = bf16[4,1024]{1,0:T(4,128)(2,1)} copy(bf16[4,1024]{1,0:T(4,128)(2,1)} %attention_step.1) | data formatting | bytes 16384

commit v3 on v2

--- a/solution.py
+++ b/solution.py
@@ -45,7 +45,7 @@
 def kernel(
     depth, q_ref, k_hbm, pos_ref, len_ref, w_hbm, out_ref,
     kbuf, wbuf, qall, qrows, keep, keep_lse,
-    send1, recv1, send2, recv2, send3, recv3, final,
+    send1, recv1, send2, recv2, final,
     k_sem, w_sem, qs_sem, qr_sem, s_sem, r_sem,
 ):
     requests, heads_here, width = q_ref.shape
@@ -69,41 +69,52 @@
     pltpu.make_async_copy(w_hbm, wbuf, w_sem).start()
 
     core_peer, row_peer = device(1, 0, 0), device(0, 1, 0)
-    level_peers = [device(0, 0, k) for k in range(1, depth)]
+    level_peers = {k: device(0, 0, k) for k in range(1, depth)}
+    owners = {(dr, k): device(0, dr, k) for dr in range(2) for k in range(depth) if dr or k}
     barrier = pltpu.get_barrier_semaphore()
-    for peer in [core_peer, row_peer] + level_peers:
+    for peer in [core_peer, row_peer] + list(level_peers.values()):
         pl.semaphore_signal(barrier, inc=1, device_id=peer, device_id_type=MESH)
     pl.semaphore_wait(barrier, depth + 1)
 
     sends, arrivals = [], {}
 
-    def send_query(src, place, peer):
+    def send_query(src, place, r, peer):
         copy = pltpu.make_async_remote_copy(
-            src_ref=src, dst_ref=qall.at[place],
-            send_sem=qs_sem.at[place], recv_sem=qr_sem.at[place],
+            src_ref=src.at[r], dst_ref=qall.at[place, r],
+            send_sem=qs_sem.at[place, r], recv_sem=qr_sem.at[place, r],
             device_id=peer, device_id_type=MESH,
         )
         copy.start()
         sends.append(copy)
-        arrivals[place] = copy
-
-    for k in range(1, depth):
-        send_query(q_ref, slot(0, 0, (depth - k) % depth), level_peers[k - 1])
-    send_query(q_ref, slot(0, 1, 0), row_peer)
-    send_query(q_ref, slot(1, 0, 0), core_peer)
+        arrivals[place, r] = copy
+
+    def gather0(r):
+        for k in range(1, depth):
+            send_query(q_ref, slot(0, 0, depth - k), r, level_peers[k])
+        send_query(q_ref, slot(0, 1, 0), r, row_peer)
+        send_query(q_ref, slot(1, 0, 0), r, core_peer)
+
+    def gather1(r):
+        for k in range(1, depth):
+            arrivals[slot(0, 0, k), r].wait_recv()
+            send_query(qall.at[slot(0, 0, k)], slot(0, 1, k), r, row_peer)
+            send_query(qall.at[slot(0, 0, k)], slot(1, 0, k), r, core_peer)
+
+    def gather2(r):
+        for k in range(depth):
+            arrivals[slot(0, 1, k), r].wait_recv()
+            send_query(qall.at[slot(0, 1, k)], slot(1, 1, k), r, core_peer)
+
+    def gather3(r):
+        for dr in range(2):
+            for k in range(depth):
+                arrivals[slot(1, dr, k), r].wait_recv()
+
+    for r in range(requests):
+        gather0(r)
     qall[0] = q_ref[...]
-    for k in range(1, depth):
-        arrivals[slot(0, 0, k)].wait_recv()
-        send_query(qall.at[slot(0, 0, k)], slot(0, 1, k), row_peer)
-        send_query(qall.at[slot(0, 0, k)], slot(1, 0, k), core_peer)
-    for k in range(depth):
-        arrivals[slot(0, 1, k)].wait_recv()
-        send_query(qall.at[slot(0, 1, k)], slot(1, 1, k), core_peer)
-    for dr in range(2):
-        for k in range(depth):
-            arrivals[slot(1, dr, k)].wait_recv()
-
-    def attend(r):
+
+    def attend(r, between=None):
         for place in range(devices):
             qrows[place * heads_here : (place + 1) * heads_here, :] = qall[place, r].astype(jnp.float32)
         pltpu.make_async_copy(k_hbm.at[r], kbuf.at[r], k_sem.at[r]).wait()
@@ -116,6 +127,8 @@
         peak = jnp.max(scores, axis=1, keepdims=True)
         weights = jnp.exp((scores - peak) * softmax_scale)
         total = jnp.sum(weights, axis=1, keepdims=True)
+        if between is not None:
+            between()
         mixed = lax.dot_general(
             weights.astype(jnp.bfloat16),
             kbuf[r, :latent, :],
@@ -134,11 +147,11 @@
         sends.append(copy)
         return copy
 
-    half, quarter = heads // 2, heads // 4
-    first, second, third = {}, {}, {}
-
-    def stage1(r):
-        mixed, lse = attend(r)
+    half = heads // 2
+    first, second = {}, {}
+
+    def reduce1(r):
+        mixed, lse = attend(r, functools.partial(reduce2, r - 1) if r else None)
         values, tail = packed(mixed[half:], lse[half:])
         send1[r, :, :latent] = values
         send1[r, :, latent:] = tail
@@ -146,46 +159,43 @@
         keep[r] = mixed[:half]
         keep_lse[r] = jnp.broadcast_to(lse[:half], (half, LANES))
 
-    def stage2(r):
+    def reduce2(r):
         first[r].wait_recv()
         mixed, lse = merge([(keep[r], keep_lse[r, :, 0:1]), unpacked(recv1.at[r], latent)])
-        values, tail = packed(mixed[quarter:], lse[quarter:])
-        send2[r, :, :latent] = values
-        send2[r, :, latent:] = tail
-        second[r] = send_part(send2.at[r], recv2.at[r], 1, r, row_peer)
-        keep[r, :quarter] = mixed[:quarter]
-        keep_lse[r, :quarter] = jnp.broadcast_to(lse[:quarter], (quarter, LANES))
-
-    def stage3(r):
-        second[r].wait_recv()
-        mixed, lse = merge(
-            [(keep[r, :quarter], keep_lse[r, :quarter, 0:1]), unpacked(recv2.at[r], latent)]
-        )
         values, tail = packed(mixed, lse)
-        for k in range(1, depth):
-            rows = slice(k * heads_here, (k + 1) * heads_here)
-            send3[r, k, :, :latent] = values[rows]
-            send3[r, k, :, latent:] = tail[rows]
-        for k in range(1, depth):
-            third[r, k] = send_part(
-                send3.at[r, k], recv3.at[r, depth - k], 1 + k, r, level_peers[k - 1]
+        for dr, k in owners:
+            place = dr * depth + k
+            rows = slice(place * heads_here, (place + 1) * heads_here)
+            send2[r, place, :, :latent] = values[rows]
+            send2[r, place, :, latent:] = tail[rows]
+        for dr, k in owners:
+            place, there = dr * depth + k, dr * depth + (depth - k) % depth
+            second[r, there] = send_part(
+                send2.at[r, place], recv2.at[r, there], there, r, owners[dr, k]
             )
         keep[r, :heads_here] = mixed[:heads_here]
         keep_lse[r, :heads_here] = jnp.broadcast_to(lse[:heads_here], (heads_here, LANES))
 
-    def stage4(r):
+    def reduce3(r):
         parts = [(keep[r, :heads_here], keep_lse[r, :heads_here, 0:1])]
-        for k in range(1, depth):
-            third[r, k].wait_recv()
-        for k in range(1, depth):
-            parts.append(unpacked(recv3.at[r, k], latent))
+        for place in range(1, 2 * depth):
+            second[r, place].wait_recv()
+        for place in range(1, 2 * depth):
+            parts.append(unpacked(recv2.at[r, place], latent))
         final[r] = merge(parts)[0]
 
-    stages = [stage1, stage2, stage3, stage4]
-    for step in range(requests + len(stages) - 1):
-        for number, stage in enumerate(stages):
-            if 0 <= step - number < requests:
-                stage(step - number)
+    order = [(gather1, 0), (gather1, 1), (gather2, 0), (gather1, 2), (gather2, 1), (gather3, 0)]
+    order = [item for item in order if item[1] < requests]
+    for r in range(requests):
+        order.append((reduce1, r))
+        later = [(gather1, r + 3), (gather2, r + 2), (gather3, r + 1)]
+        order += [item for item in later if item[1] < requests]
+        if r > 1:
+            order.append((reduce3, r - 2))
+    order += [(reduce2, requests - 1)]
+    order += [(reduce3, r) for r in range(max(requests - 2, 0), requests)]
+    for stage, r in order:
+        stage(r)
 
     pltpu.make_async_copy(w_hbm, wbuf, w_sem).wait()
     for h in range(heads_here):
@@ -204,7 +214,7 @@
     latent, value = value_up.shape[1:]
     heads = devices * heads_here
     wide = latent + LANES
-    half, quarter = heads // 2, heads // 4
+    half = heads // 2
     vmem = pl.BlockSpec(memory_space=pltpu.VMEM)
     hbm = pl.BlockSpec(memory_space=pltpu.HBM)
     bf16, f32 = jnp.bfloat16, jnp.float32
@@ -222,17 +232,15 @@
             pltpu.VMEM((requests, half, LANES), f32),
             pltpu.VMEM((requests, half, wide), bf16),
             pltpu.VMEM((requests, half, wide), bf16),
-            pltpu.VMEM((requests, quarter, wide), bf16),
-            pltpu.VMEM((requests, quarter, wide), bf16),
-            pltpu.VMEM((requests, depth, heads_here, wide), bf16),
-            pltpu.VMEM((requests, depth, heads_here, wide), bf16),
+            pltpu.VMEM((requests, 2 * depth, heads_here, wide), bf16),
+            pltpu.VMEM((requests, 2 * depth, heads_here, wide), bf16),
             pltpu.VMEM((requests, heads_here, latent), f32),
             pltpu.SemaphoreType.DMA((requests,)),
             pltpu.SemaphoreType.DMA,
-            pltpu.SemaphoreType.DMA((devices,)),
-            pltpu.SemaphoreType.DMA((devices,)),
-            pltpu.SemaphoreType.DMA((1 + depth, requests)),
-            pltpu.SemaphoreType.DMA((1 + depth, requests)),
+            pltpu.SemaphoreType.DMA((devices, requests)),
+            pltpu.SemaphoreType.DMA((devices, requests)),
+            pltpu.SemaphoreType.DMA((2 * depth, requests)),
+            pltpu.SemaphoreType.DMA((2 * depth, requests)),
         ],
         compiler_params=pltpu.CompilerParams(
             collective_id=0, has_side_effects=True, vmem_limit_bytes=56 * 1024 * 1024

time: 35.5 us -> 32.8 us (0.924)
  Pallas kernels: 34 us -> 31.3 us
    pallas_call x1, Pallas kernels: 34 us -> 31.3 us  [shards(): pl.pallas_call(functools.partial(kernel, depth), out_shape=jax.ShapeDtype...]
where the time goes in v3:
time: 32.8 us; the launch traced here: 32.6 us
  Pallas kernels  31.3 us (95%)
  local copies, waits for them, and re-layouts  1.3 us (4%)
    pallas_call x1, Pallas kernels, shards(): pl.pallas_call(functools.partial(kernel, depth), out_shape=jax.ShapeDtype...  31.3 us
    unnamed x1, local copies, waits for them, and re-layouts  1.3 us

profile of v3, /device:TPU:0, one launch (start us, length us, event | category | flops | bytes accessed | tf_op | source)
XLA Modules:
  0.0 32.6 jit_solution(8557775124634035022)
XLA Ops:
  0.0 31.3 %attention_step.1 = bf16[4,1024]{1,0:T(4,128)(2,1)} custom-call(bf16[4,8,576]{2,1,0:T(8,128)(2,1)} %q_ref.1, bf16[4,576,2048]{2,1,0:T(8,128)(2,1)} %bitcast.1, s32[4,2048]{1,0:T(4,128)} %pos_ref.1, s32[4]{0:T(128)} %len_ref.1, bf16[8,512,128]{2,1,0:T(8,128)(2,1)} %w_hbm.1), custom_call_target="tpu_custom_call" | custom-call | tf_op jit(solution)/shard_map/attention_step/pallas_call | solution.py:221
  31.3 1.3 %copy.7 = bf16[4,1024]{1,0:T(4,128)(2,1)} copy(bf16[4,1024]{1,0:T(4,128)(2,1)} %attention_step.1) | data formatting | bytes 16384

commit v4 on v3

--- a/solution.py
+++ b/solution.py
@@ -168,7 +168,7 @@
             rows = slice(place * heads_here, (place + 1) * heads_here)
             send2[r, place, :, :latent] = values[rows]
             send2[r, place, :, latent:] = tail[rows]
-        for dr, k in owners:
+        for dr, k in sorted(owners, key=lambda o: -(o[0] + min(o[1], depth - o[1]))):
             place, there = dr * depth + k, dr * depth + (depth - k) % depth
             second[r, there] = send_part(
                 send2.at[r, place], recv2.at[r, there], there, r, owners[dr, k]

time: 32.8 us -> 32.6 us (level)
  no operation moved by 1% of the time
where the time goes in v4:
time: 32.6 us; the launch traced here: 32.4 us
  Pallas kernels  31.1 us (95%)
  local copies, waits for them, and re-layouts  1.3 us (4%)
    pallas_call x1, Pallas kernels, shards(): pl.pallas_call(functools.partial(kernel, depth), out_shape=jax.ShapeDtype...  31.1 us
    unnamed x1, local copies, waits for them, and re-layouts  1.3 us

profile of v4, /device:TPU:0, one launch (start us, length us, event | category | flops | bytes accessed | tf_op | source)
XLA Modules:
  0.0 32.4 jit_solution(195926943175710418)
XLA Ops:
  0.0 31.1 %attention_step.1 = bf16[4,1024]{1,0:T(4,128)(2,1)} custom-call(bf16[4,8,576]{2,1,0:T(8,128)(2,1)} %q_ref.1, bf16[4,576,2048]{2,1,0:T(8,128)(2,1)} %bitcast.1, s32[4,2048]{1,0:T(4,128)} %pos_ref.1, s32[4]{0:T(128)} %len_ref.1, bf16[8,512,128]{2,1,0:T(8,128)(2,1)} %w_hbm.1), custom_call_target="tpu_custom_call" | custom-call | tf_op jit(solution)/shard_map/attention_step/pallas_call | solution.py:221
  31.1 1.3 %copy.7 = bf16[4,1024]{1,0:T(4,128)(2,1)} copy(bf16[4,1024]{1,0:T(4,128)(2,1)} %attention_step.1) | data formatting | bytes 16384
